TPU v7x, 32 devices: a whole 2x2x4 slice. The times are simulated.
32 devices in a mesh: gx: 8 (over z, core), gy: 4 (over y, x).
Axes of the slice: x: 2, y: 2, z: 4, core: 2. Of those that a mesh axis runs over, the one named last changes fastest.
Arguments:
- points: bfloat16 [64, 65536], P(None, ('gx', 'gy')), may hold values from -6 to 6
- vectors: bfloat16 [32, 65536], P(None, ('gx', 'gy')), may hold values from -6 to 6
- leaf_pick: int32 [128, 128], P(('gx', 'gy')), may hold values from 0 to 511
- leaf_assign: int32 [128, 512], P(('gx', 'gy')), may hold values from 0 to 127
- device_pick: int32 [32, 128], P(('gx', 'gy')), may hold values from 0 to 511
- device_assign: int32 [32, 512], P(('gx', 'gy')), may hold values from 0 to 127
- node_pick: int32 [8, 3, 128], P('gx'), may hold values from 0 to 255
- node_assign: int32 [8, 3, 256], P('gx'), may hold values from 0 to 127
- far_mask: int32 [8, 8], P('gx'), may hold values from 0 to 1, as said below
- near_lower: int32 [32, 4, 12], P(('gx', 'gy')), may hold values from -1 to 3, as said below
- near_upper: int32 [32, 4, 12], P(('gx', 'gy')), may hold values from 0 to 3, as said below
Outputs:
- potential: float32 [32, 65536], P(None, ('gx', 'gy'))
Inputs may be any that keep to these rules, and one draw needn't show every extreme that they name: near_lower[d, o, j] is a local leaf of device d forming a near pair with local leaf near_upper[d, o, j] of device d + o + 1, or -1 for an empty slot; the slots of one d and o never name the same pair of leaves, and no live slot names a device past the last. `near_upper`: A local leaf of device d + o + 1, read only where near_lower is live. `far_mask`: Symmetric, zero on the diagonal, one where the two group indices differ by exactly 1.
All inputs are finite; a program needn't handle non-finite values.
Results may differ from a plain program's by a relative error of at most 0.0015.
Values may be sent and summed in bfloat16 or wider, within the bound.
No kernel may reach another device: no remote copies, remote signals or barrier semaphores. Data moves between devices by JAX's collectives and lax.ppermute only.
A program may use at most 128 MiB of HBM per device.

v0:
```python
import jax
import jax.numpy as jnp
from jax import lax
from jax.sharding import PartitionSpec as P

DIM = 64
COLS = 32
LEAF = 512
SKEL = 128
LPD = 4
KERNEL_RATE = 2.0


def passed_along(value, axis, steps):
    count = lax.axis_size(axis)
    first, last = (max(0, -steps), min(count, count - steps))
    return lax.ppermute(value, axis, [(source, source + steps) for source in range(first, last)])


def from_partner(value, axis, bit):
    mask = 2**bit
    pairs = [(source, source ^ mask) for source in range(lax.axis_size(axis))]
    return lax.ppermute(value, axis, pairs)


def kernel_block(source, target):
    decay_rate = KERNEL_RATE / source.shape[0]
    source_wide = source.astype(jnp.float32)
    target_wide = target.astype(jnp.float32)
    source_norm = jnp.sum(source_wide * source_wide, axis=0)
    target_norm = jnp.sum(target_wide * target_wide, axis=0)
    products = lax.dot_general(
        source, target, (((0,), (0,)), ((), ())), preferred_element_type=jnp.float32
    )
    return jnp.exp(-decay_rate * (source_norm[:, None] + target_norm[None, :] - 2.0 * products))


def add_columns(running, terms, first_col):
    current = lax.dynamic_slice_in_dim(running, first_col, terms.shape[1], 1)
    return lax.dynamic_update_slice_in_dim(running, current + terms, first_col, 1)


def pick_columns(table_matrix, col_index):
    return jnp.take(table_matrix, col_index, axis=1)


def one_hot(assignment, width_count):
    return (assignment[:, None] == jnp.arange(width_count, dtype=jnp.int32)[None, :]).astype(
        jnp.float32
    )


def pair_terms(low_points, low_values, high_points, high_values):
    kernel_tile = kernel_block(low_points, high_points).astype(jnp.bfloat16)
    to_upper = jnp.dot(low_values, kernel_tile, preferred_element_type=jnp.float32)
    to_lower = lax.dot_general(
        high_values, kernel_tile, (((1,), (1,)), ((), ())), preferred_element_type=jnp.float32
    )
    return (to_lower, to_upper)


def neighbour_terms(
    offset,
    near_lower,
    near_upper,
    points,
    columns,
    high_block,
    high_columns,
    near_terms,
    upper_terms,
):
    for slot_index in range(near_lower.shape[2]):
        lower_leaf = near_lower[0, offset - 1, slot_index]
        upper_leaf = near_upper[0, offset - 1, slot_index]
        live_flag = lower_leaf >= 0
        lower_col = jnp.maximum(lower_leaf, 0) * LEAF
        upper_col = upper_leaf * LEAF
        low_points = lax.dynamic_slice_in_dim(points, lower_col, LEAF, 1)
        low_values = lax.dynamic_slice_in_dim(columns, lower_col, LEAF, 1)
        high_points = lax.dynamic_slice_in_dim(high_block, upper_col, LEAF, 1)
        high_values = lax.dynamic_slice_in_dim(high_columns, upper_col, LEAF, 1)
        to_lower, to_upper = pair_terms(low_points, low_values, high_points, high_values)
        live_scale = live_flag.astype(jnp.float32)
        to_lower = to_lower * live_scale
        to_upper = to_upper * live_scale
        near_terms = add_columns(near_terms, to_lower, lower_col)
        upper_terms = add_columns(upper_terms, to_upper, upper_col)
    return (near_terms, upper_terms)


def on_device(
    points,
    vectors,
    leaf_pick,
    leaf_assign,
    device_pick,
    device_assign,
    node_pick,
    node_assign,
    far_mask,
    near_lower,
    near_upper,
):
    device_cols = points.shape[1]
    reach_count = lax.axis_size("gy")
    levels = reach_count.bit_length() - 1
    row_index = lax.axis_index("gy")

    def self_target(target, running):
        first_col = target * LEAF
        target_points = lax.dynamic_slice_in_dim(points, first_col, LEAF, 1)
        kernel_tile = kernel_block(points, target_points).astype(jnp.bfloat16)
        self_terms = jnp.dot(vectors, kernel_tile, preferred_element_type=jnp.float32)
        return lax.dynamic_update_slice_in_dim(running, self_terms, first_col, 1)

    near_terms = lax.fori_loop(0, LPD, self_target, jnp.zeros((COLS, device_cols), jnp.float32))
    for offset in range(1, reach_count + 1):
        high_block, high_columns = passed_along((points, vectors), ("gx", "gy"), -offset)
        upper_terms = jnp.zeros((COLS, device_cols), jnp.float32)
        near_terms, upper_terms = neighbour_terms(
            offset,
            near_lower,
            near_upper,
            points,
            vectors,
            high_block,
            high_columns,
            near_terms,
            upper_terms,
        )
        near_terms = near_terms + passed_along(upper_terms, ("gx", "gy"), offset)
    leaf_points = points.reshape(DIM, LPD, LEAF)
    leaf_values = vectors.reshape(COLS, LPD, LEAF)
    skeleton_points = jax.vmap(pick_columns, in_axes=(1, 0))(leaf_points, leaf_pick)
    leaf_onehot = leaf_assign[:, :, None] == jnp.arange(SKEL, dtype=jnp.int32)[None, None, :]
    leaf_weights = jnp.einsum(
        "cln,lns->lcs",
        leaf_values,
        leaf_onehot.astype(jnp.bfloat16),
        preferred_element_type=jnp.float32,
    )
    joined_points = skeleton_points.transpose(1, 0, 2).reshape(DIM, LPD * SKEL)
    joined_weights = leaf_weights.transpose(1, 0, 2).reshape(COLS, LPD * SKEL)
    node_points = jnp.take(joined_points, device_pick[0], axis=1)
    device_onehot = one_hot(device_assign[0], SKEL)
    node_weights = jnp.dot(joined_weights, device_onehot, precision=lax.Precision.HIGHEST)
    path_onehots = []
    for level_index in range(1, levels + 1):
        heap_index = (reach_count >> level_index) - 1 + (row_index >> level_index)
        assignment = lax.dynamic_index_in_dim(node_assign[0], heap_index, 0, keepdims=False)
        path_onehots.append(one_hot(assignment, SKEL))
    for level_index in range(1, levels + 1):
        bit_index = level_index - 1
        other_points = from_partner(node_points, "gy", bit_index)
        other_weights = from_partner(node_weights, "gy", bit_index)
        upper_side = row_index >> bit_index & 1 == 1
        pair_points = jnp.where(
            upper_side,
            jnp.concatenate([other_points, node_points], 1),
            jnp.concatenate([node_points, other_points], 1),
        )
        pair_weights = jnp.where(
            upper_side,
            jnp.concatenate([other_weights, node_weights], 1),
            jnp.concatenate([node_weights, other_weights], 1),
        )
        heap_index = (reach_count >> level_index) - 1 + (row_index >> level_index)
        node_picks = lax.dynamic_index_in_dim(node_pick[0], heap_index, 0, keepdims=False)
        node_points = jnp.take(pair_points, node_picks, axis=1)
        node_weights = jnp.dot(
            pair_weights, path_onehots[level_index - 1], precision=lax.Precision.HIGHEST
        )
    gathered_roots = lax.all_gather(node_points[None], "gx", axis=0, tiled=True)
    far_flags = far_mask[0].astype(jnp.float32)
    root_kernels = jax.vmap(kernel_block, in_axes=(0, None))(gathered_roots, node_points)
    node_potential = jnp.einsum(
        "n,ncs,nst->ct",
        far_flags,
        lax.all_gather(node_weights[None], "gx", axis=0, tiled=True),
        root_kernels,
        precision=lax.Precision.HIGHEST,
    )
    for level_index in range(levels, 0, -1):
        child_potential = jnp.dot(
            node_potential, path_onehots[level_index - 1].T, precision=lax.Precision.HIGHEST
        )
        child_side = row_index >> level_index - 1 & 1
        node_potential = lax.dynamic_slice_in_dim(child_potential, child_side * SKEL, SKEL, 1)
    leaf_joined = jnp.dot(node_potential, device_onehot.T, precision=lax.Precision.HIGHEST).reshape(
        COLS, LPD, SKEL
    )
    far_terms = jnp.einsum(
        "cls,lns->cln",
        leaf_joined,
        leaf_onehot.astype(jnp.float32),
        precision=lax.Precision.HIGHEST,
    ).reshape(COLS, device_cols)
    return near_terms + far_terms


def solution(mesh):
    placed = (
        P(None, ("gx", "gy")),
        P(None, ("gx", "gy")),
        P(("gx", "gy"), None),
        P(("gx", "gy"), None),
        P(("gx", "gy"), None),
        P(("gx", "gy"), None),
        P("gx", None, None),
        P("gx", None, None),
        P("gx", None),
        P(("gx", "gy"), None, None),
        P(("gx", "gy"), None, None),
    )
    return jax.shard_map(
        on_device, mesh=mesh, in_specs=placed, out_specs=P(None, ("gx", "gy")), check_vma=False
    )
```

profile of v0, /device:TPU:5, one launch (start us, length us, event | category | flops | bytes accessed | tf_op | source)
XLA Modules:
  0.0 233.5 jit_solution(3398589110747293190)
XLA Ops:
  0.0 3.2 %collective-permute-start.1 = (bf16[64,2048]{1,0:T(8,128)(2,1)}, bf16[64,2048]{1,0:T(8,128)(2,1)S(1)}, u32[]{:S(2)}, u32[]{:S(2)}) collective-permute-start(bf16[64,2048]{1,0:T(8,128)(2,1)} %param.15), channel_id=1, source_target_pairs={{1,0},{2,1},{3,2},{4,3},{5,4},{6,5},{7,6},{8,7},{9,8},{10,9},{11,1... | collective-permute-start | bytes 786440 | tf_op jit(solution)/shard_map/ppermute | solution.py:17
  3.2 3.7 %collective-permute-start.4 = (bf16[64,2048]{1,0:T(8,128)(2,1)}, bf16[64,2048]{1,0:T(8,128)(2,1)S(1)}, u32[]{:S(2)}, u32[]{:S(2)}) collective-permute-start(bf16[64,2048]{1,0:T(8,128)(2,1)} %param.15), channel_id=1, source_target_pairs={{2,0},{3,1},{4,2},{5,3},{6,4},{7,5},{8,6},{9,7},{10,8},{11,9},{12,... | collective-permute-start | bytes 786440 | tf_op jit(solution)/shard_map/ppermute | solution.py:17
  6.9 2.4 %collective-permute-start = (bf16[32,2048]{1,0:T(8,128)(2,1)}, bf16[32,2048]{1,0:T(8,128)(2,1)S(1)}, u32[]{:S(2)}, u32[]{:S(2)}) collective-permute-start(bf16[32,2048]{1,0:T(8,128)(2,1)} %param.16), channel_id=1, source_target_pairs={{1,0},{2,1},{3,2},{4,3},{5,4},{6,5},{7,6},{8,7},{9,8},{10,9},{11,1... | collective-permute-start | bytes 393224 | tf_op jit(solution)/shard_map/ppermute | solution.py:17
  9.4 1.9 collective-permute-start.3
  11.3 1.2 copy.24
  12.7 3.2 %gather_fusion.1 = bf16[512,64]{1,0:T(8,128)(2,1)S(1)} fusion(bf16[4,64,512]{1,2,0:T(8,128)(2,1)S(1)} %bitcast.341, s32[512]{0:T(512)S(1)} %fusion.383), kind=kCustom, calls=%fused_computation.3 | custom fusion | bytes 135168 | tf_op jit(solution)/shard_map/vmap(jit(_take))/gather | solution.py:44
  16.0 0.7 gather_fusion
  16.8 1.5 collective-permute-start.14
  18.3 0.7 fusion.396
  19.6 0.7 fusion.392
  22.3 0.7 fusion.393
  28.7 0.7 fusion.395
  52.0 0.7 fusion.394
  70.5 0.7 fusion.391
  112.8 6.5 %while.13 = (s32[]{:T(128)}, f32[32,2048]{1,0:T(8,128)S(1)}, bf16[64,2048]{1,0:T(8,128)(2,1)S(1)}, bf16[32,2048]{1,0:T(8,128)(2,1)S(1)}, s32[]{:T(128)}, /*index=5*/s32[]{:T(128)}, s32[]{:T(128)}, s32[]{:T(128)}) while((s32[]{:T(128)}, f32[32,2048]{1,0:T(8,128)S(1)}, bf16[64,2048]{1,0:T(8,128)(2,1)S(1)}, bf16[32,2048]{1,0:T(8,128)(2,1)S(1)}, ...), condition=%wide.region_3.0_spmd, body=%wide.region_0.0_spmd.sunk | while | flops 207058432 | bytes 873615 | solution.py:117
  113.0 1.5 fusion.505
  114.6 1.5 fusion.505
  116.2 1.5 fusion.505
  117.9 1.5 fusion.505
  119.6 0.7 convolution_bitcast_fusion.2
  122.3 0.7 gather_fusion.2
  123.1 1.7 collective-permute-done.12
  125.3 2.2 collective-permute-done.15
  127.6 0.7 collective-permute-start.13
  128.3 0.7 gather_fusion.3
  129.3 17.5 %all-gather.1 = bf16[512,128]{1,0:T(8,128)(2,1)S(1)} all-gather(bf16[64,128]{1,0:T(8,128)(2,1)S(1)} %copy.25), channel_id=3, replica_groups=mesh['gx'=8,'gy'=4] {'gx'}, dimensions={0}, use_global_device_ids=true | all-gather | bytes 147456 | tf_op jit(solution)/shard_map/all_gather | solution.py:174
  146.8 2.6 %collective-permute-start.7 = (bf16[64,2048]{1,0:T(8,128)(2,1)S(1)}, bf16[64,2048]{1,0:T(8,128)(2,1)S(1)}, u32[]{:S(2)}, u32[]{:S(2)}) collective-permute-start(bf16[64,2048]{1,0:T(8,128)(2,1)S(1)} %get-tuple-element.348), channel_id=1, source_target_pairs={{3,0},{4,1},{5,2},{6,3},{7,4},{8,5},{9,6},{10,7},{11,8},{12,9},{13... | collective-permute-start | bytes 786440 | tf_op jit(solution)/shard_map/ppermute | solution.py:17
  149.7 14.9 %all-gather = f32[256,128]{1,0:T(8,128)S(1)} all-gather(f32[32,128]{1,0:T(8,128)S(1)} %fusion.308), channel_id=2, replica_groups=mesh['gx'=8,'gy'=4] {'gx'}, dimensions={0}, use_global_device_ids=true | all-gather | bytes 147456 | tf_op jit(solution)/shard_map/all_gather | solution.py:180
  166.3 1.0 convolution_bitcast_fusion
  167.4 2.2 collective-permute-start.6
  177.4 1.9 collective-permute-start.10
  183.3 0.4 fusion.185
  185.8 0.4 fusion.181
  187.1 2.1 collective-permute-start.9
  190.1 0.4 fusion.178
  192.0 0.4 fusion.175
  193.9 0.4 fusion.172
  195.7 0.4 fusion.169
  196.4 0.4 fusion.168
  197.0 3.5 %collective-permute-start.2 = (f32[32,2048]{1,0:T(8,128)S(1)}, f32[32,2048]{1,0:T(8,128)S(1)}, u32[]{:S(2)}, u32[]{:S(2)}) collective-permute-start(f32[32,2048]{1,0:T(8,128)S(1)} %fusion.234), channel_id=1, source_target_pairs={{0,1},{1,2},{2,3},{3,4},{4,5},{5,6},{6,7},{7,8},{8,9},{9,10},{10,1... | collective-permute-start | bytes 786440 | tf_op jit(solution)/shard_map/ppermute | solution.py:17
  202.1 0.4 fusion.165
  202.7 0.4 fusion.164
  203.9 0.4 fusion.162
  206.4 0.4 fusion.158
  208.3 4.5 %collective-permute-start.5 = (f32[32,2048]{1,0:T(8,128)S(1)}, f32[32,2048]{1,0:T(8,128)S(1)}, u32[]{:S(2)}, u32[]{:S(2)}) collective-permute-start(f32[32,2048]{1,0:T(8,128)S(1)} %fusion.256), channel_id=1, source_target_pairs={{0,2},{1,3},{2,4},{3,5},{4,6},{5,7},{6,8},{7,9},{8,10},{9,11},{10,... | collective-permute-start | bytes 786440 | tf_op jit(solution)/shard_map/ppermute | solution.py:17
  216.1 3.4 %collective-permute-start.8 = (f32[32,2048]{1,0:T(8,128)S(1)}, f32[32,2048]{1,0:T(8,128)S(1)}, u32[]{:S(2)}, u32[]{:S(2)}) collective-permute-start(f32[32,2048]{1,0:T(8,128)S(1)} %fusion.278), channel_id=1, source_target_pairs={{0,3},{1,4},{2,5},{3,6},{4,7},{5,8},{6,9},{7,10},{8,11},{9,12},{10... | collective-permute-start | bytes 786440 | tf_op jit(solution)/shard_map/ppermute | solution.py:17
  219.6 3.3 %collective-permute-start.11 = (f32[32,2048]{1,0:T(8,128)S(1)}, f32[32,2048]{1,0:T(8,128)S(1)}, u32[]{:S(2)}, u32[]{:S(2)}) collective-permute-start(f32[32,2048]{1,0:T(8,128)S(1)} %fusion.300), channel_id=1, source_target_pairs={{0,4},{1,5},{2,6},{3,7},{4,8},{5,9},{6,10},{7,11},{8,12},{9,13},{1... | collective-permute-start | bytes 786440 | tf_op jit(solution)/shard_map/ppermute | solution.py:17
  232.7 0.8 add_add_fusion
  (220 shorter events, 43.3 us)
Async XLA Ops:
  0.0 12.6 %copy-start.4 = (s32[4,128]{1,0:T(4,128)S(1)}, s32[4,128]{1,0:T(4,128)}, u32[]{:S(2)}) copy-start(s32[4,128]{1,0:T(4,128)} %param.17) | copy-start | bytes 6148
  0.0 12.6 %copy-start.8 = (s32[1,128]{1,0:T(1,128)S(1)}, s32[1,128]{1,0:T(1,128)}, u32[]{:S(2)}) copy-start(s32[1,128]{1,0:T(1,128)} %param.19) | copy-start | bytes 1540
  0.0 167.4 %collective-permute-start.1 = (bf16[64,2048]{1,0:T(8,128)(2,1)}, bf16[64,2048]{1,0:T(8,128)(2,1)S(1)}, u32[]{:S(2)}, u32[]{:S(2)}) collective-permute-start(bf16[64,2048]{1,0:T(8,128)(2,1)} %param.15), channel_id=1, source_target_pairs={{1,0},{2,1},{3,2},{4,3},{5,4},{6,5},{7,6},{8,7},{9,8},{10,9},{11,1... | collective-permute-start | bytes 786440 | tf_op jit(solution)/shard_map/ppermute | solution.py:17
  3.2 174.2 %collective-permute-start.4 = (bf16[64,2048]{1,0:T(8,128)(2,1)}, bf16[64,2048]{1,0:T(8,128)(2,1)S(1)}, u32[]{:S(2)}, u32[]{:S(2)}) collective-permute-start(bf16[64,2048]{1,0:T(8,128)(2,1)} %param.15), channel_id=1, source_target_pairs={{2,0},{3,1},{4,2},{5,3},{6,4},{7,5},{8,6},{9,7},{10,8},{11,9},{12,... | collective-permute-start | bytes 786440 | tf_op jit(solution)/shard_map/ppermute | solution.py:17
  6.9 201.4 %collective-permute-start = (bf16[32,2048]{1,0:T(8,128)(2,1)}, bf16[32,2048]{1,0:T(8,128)(2,1)S(1)}, u32[]{:S(2)}, u32[]{:S(2)}) collective-permute-start(bf16[32,2048]{1,0:T(8,128)(2,1)} %param.16), channel_id=1, source_target_pairs={{1,0},{2,1},{3,2},{4,3},{5,4},{6,5},{7,6},{8,7},{9,8},{10,9},{11,1... | collective-permute-start | bytes 393224 | tf_op jit(solution)/shard_map/ppermute | solution.py:17
  9.4 210.2 %collective-permute-start.3 = (bf16[32,2048]{1,0:T(8,128)(2,1)}, bf16[32,2048]{1,0:T(8,128)(2,1)S(1)}, u32[]{:S(2)}, u32[]{:S(2)}) collective-permute-start(bf16[32,2048]{1,0:T(8,128)(2,1)} %param.16), channel_id=1, source_target_pairs={{2,0},{3,1},{4,2},{5,3},{6,4},{7,5},{8,6},{9,7},{10,8},{11,9},{12,... | collective-permute-start | bytes 393224 | tf_op jit(solution)/shard_map/ppermute | solution.py:17
  12.6 4.1 %copy-start.7 = (s32[1,3,128]{2,0,1:T(1,128)S(1)}, s32[1,3,128]{2,0,1:T(1,128)}, u32[]{:S(2)}) copy-start(s32[1,3,128]{2,0,1:T(1,128)} %param.21) | copy-start | bytes 4612
  12.6 5.7 %copy-start.2 = (s32[1,4,12]{2,1,0:T(4,128)S(1)}, s32[1,4,12]{2,1,0:T(4,128)}, u32[]{:S(2)}) copy-start(s32[1,4,12]{2,1,0:T(4,128)} %param.24) | copy-start | bytes 580
  12.7 6.9 %copy-start.3 = (s32[1,4,12]{2,1,0:T(4,128)S(1)}, s32[1,4,12]{2,1,0:T(4,128)}, u32[]{:S(2)}) copy-start(s32[1,4,12]{2,1,0:T(4,128)} %param.25) | copy-start | bytes 580
  16.8 105.3 %collective-permute-start.14 = (bf16[64,128]{0,1:T(8,128)(2,1)S(1)}, bf16[64,128]{0,1:T(8,128)(2,1)S(1)}, u32[]{:S(2)}, u32[]{:S(2)}) collective-permute-start(bf16[64,128]{0,1:T(8,128)(2,1)S(1)} %select_bitcast_fusion.1), channel_id=1, source_target_pairs={{0,1},{1,0},{2,3},{3,2},{4,5},{5,4},{6,7},{7,6},{8,9},{9,8},{10,11... | collective-permute-start | bytes 49160 | tf_op jit(solution)/shard_map/ppermute | solution.py:23
  28.6 84.1 %copy-start.6 = (s32[1,3,256]{2,0,1:T(1,128)S(1)}, s32[1,3,256]{2,0,1:T(1,128)}, u32[]{:S(2)}) copy-start(s32[1,3,256]{2,0,1:T(1,128)} %param.22) | copy-start | bytes 9220
  29.4 83.4 %copy-start.10 = (s32[1,8]{1,0:T(1,128)S(1)}, s32[1,8]{1,0:T(1,128)}, u32[]{:S(2)}) copy-start(s32[1,8]{1,0:T(1,128)} %param.23) | copy-start | bytes 100
  50.6 62.2 %copy-start = (bf16[64,2048]{1,0:T(8,128)(2,1)S(1)}, bf16[64,2048]{1,0:T(8,128)(2,1)}, u32[]{:S(2)}) copy-start(bf16[64,2048]{1,0:T(8,128)(2,1)} %param.15) | copy-start | bytes 786436
  50.6 62.2 %copy-start.1 = (bf16[32,2048]{1,0:T(8,128)(2,1)S(1)}, bf16[32,2048]{1,0:T(8,128)(2,1)}, u32[]{:S(2)}) copy-start(bf16[32,2048]{1,0:T(8,128)(2,1)} %param.16) | copy-start | bytes 393220
  112.8 6.7 %copy-start.9 = (s32[4,512]{1,0:T(4,128)S(1)}, s32[4,512]{1,0:T(4,128)}, u32[]{:S(2)}) copy-start(s32[4,512]{1,0:T(4,128)} %param.18) | copy-start | bytes 24580
  119.4 0.9 copy-start.5
  122.2 2.7 %collective-permute-start.12 = (f32[32,128]{1,0:T(8,128)S(1)}, f32[32,128]{1,0:T(8,128)S(1)}, u32[]{:S(2)}, u32[]{:S(2)}) collective-permute-start(f32[32,128]{1,0:T(8,128)S(1)} %fusion.303), channel_id=1, source_target_pairs={{0,1},{1,0},{2,3},{3,2},{4,5},{5,4},{6,7},{7,6},{8,9},{9,8},{10,11... | collective-permute-start | bytes 49160 | tf_op jit(solution)/shard_map/ppermute | solution.py:23
  124.8 2.8 %collective-permute-start.15 = (bf16[64,128]{0,1:T(8,128)(2,1)S(1)}, bf16[64,128]{0,1:T(8,128)(2,1)S(1)}, u32[]{:S(2)}, u32[]{:S(2)}) collective-permute-start(bf16[64,128]{0,1:T(8,128)(2,1)S(1)} %select_bitcast_fusion), channel_id=1, source_target_pairs={{0,2},{1,3},{2,0},{3,1},{4,6},{5,7},{6,4},{7,5},{8,10},{9,11},{10,... | collective-permute-start | bytes 49160 | tf_op jit(solution)/shard_map/ppermute | solution.py:23
  127.6 19.2 %collective-permute-start.13 = (f32[32,128]{1,0:T(8,128)S(1)}, f32[32,128]{1,0:T(8,128)S(1)}, u32[]{:S(2)}, u32[]{:S(2)}) collective-permute-start(f32[32,128]{1,0:T(8,128)S(1)} %fusion.310), channel_id=1, source_target_pairs={{0,2},{1,3},{2,0},{3,1},{4,6},{5,7},{6,4},{7,5},{8,10},{9,11},{10,... | collective-permute-start | bytes 49160 | tf_op jit(solution)/shard_map/ppermute | solution.py:23
  146.8 40.2 %collective-permute-start.7 = (bf16[64,2048]{1,0:T(8,128)(2,1)S(1)}, bf16[64,2048]{1,0:T(8,128)(2,1)S(1)}, u32[]{:S(2)}, u32[]{:S(2)}) collective-permute-start(bf16[64,2048]{1,0:T(8,128)(2,1)S(1)} %get-tuple-element.348), channel_id=1, source_target_pairs={{3,0},{4,1},{5,2},{6,3},{7,4},{8,5},{9,6},{10,7},{11,8},{12,9},{13... | collective-permute-start | bytes 786440 | tf_op jit(solution)/shard_map/ppermute | solution.py:17
  167.4 58.8 %collective-permute-start.6 = (bf16[32,2048]{1,0:T(8,128)(2,1)S(1)}, bf16[32,2048]{1,0:T(8,128)(2,1)S(1)}, u32[]{:S(2)}, u32[]{:S(2)}) collective-permute-start(bf16[32,2048]{1,0:T(8,128)(2,1)S(1)} %get-tuple-element.353), channel_id=1, source_target_pairs={{3,0},{4,1},{5,2},{6,3},{7,4},{8,5},{9,6},{10,7},{11,8},{12,9},{13... | collective-permute-start | bytes 393224 | tf_op jit(solution)/shard_map/ppermute | solution.py:17
  177.4 19.6 %collective-permute-start.10 = (bf16[64,2048]{1,0:T(8,128)(2,1)S(1)}, bf16[64,2048]{1,0:T(8,128)(2,1)S(1)}, u32[]{:S(2)}, u32[]{:S(2)}) collective-permute-start(bf16[64,2048]{1,0:T(8,128)(2,1)S(1)} %get-tuple-element.348), channel_id=1, source_target_pairs={{4,0},{5,1},{6,2},{7,3},{8,4},{9,5},{10,6},{11,7},{12,8},{13,9},{1... | collective-permute-start | bytes 786440 | tf_op jit(solution)/shard_map/ppermute | solution.py:17
  187.1 42.4 %collective-permute-start.9 = (bf16[32,2048]{1,0:T(8,128)(2,1)S(1)}, bf16[32,2048]{1,0:T(8,128)(2,1)S(1)}, u32[]{:S(2)}, u32[]{:S(2)}) collective-permute-start(bf16[32,2048]{1,0:T(8,128)(2,1)S(1)} %get-tuple-element.353), channel_id=1, source_target_pairs={{4,0},{5,1},{6,2},{7,3},{8,4},{9,5},{10,6},{11,7},{12,8},{13,9},{1... | collective-permute-start | bytes 393224 | tf_op jit(solution)/shard_map/ppermute | solution.py:17
  197.0 19.1 %collective-permute-start.2 = (f32[32,2048]{1,0:T(8,128)S(1)}, f32[32,2048]{1,0:T(8,128)S(1)}, u32[]{:S(2)}, u32[]{:S(2)}) collective-permute-start(f32[32,2048]{1,0:T(8,128)S(1)} %fusion.234), channel_id=1, source_target_pairs={{0,1},{1,2},{2,3},{3,4},{4,5},{5,6},{6,7},{7,8},{8,9},{9,10},{10,1... | collective-permute-start | bytes 786440 | tf_op jit(solution)/shard_map/ppermute | solution.py:17
  208.3 17.8 %collective-permute-start.5 = (f32[32,2048]{1,0:T(8,128)S(1)}, f32[32,2048]{1,0:T(8,128)S(1)}, u32[]{:S(2)}, u32[]{:S(2)}) collective-permute-start(f32[32,2048]{1,0:T(8,128)S(1)} %fusion.256), channel_id=1, source_target_pairs={{0,2},{1,3},{2,4},{3,5},{4,6},{5,7},{6,8},{7,9},{8,10},{9,11},{10,... | collective-permute-start | bytes 786440 | tf_op jit(solution)/shard_map/ppermute | solution.py:17
  216.1 13.3 %collective-permute-start.8 = (f32[32,2048]{1,0:T(8,128)S(1)}, f32[32,2048]{1,0:T(8,128)S(1)}, u32[]{:S(2)}, u32[]{:S(2)}) collective-permute-start(f32[32,2048]{1,0:T(8,128)S(1)} %fusion.278), channel_id=1, source_target_pairs={{0,3},{1,4},{2,5},{3,6},{4,7},{5,8},{6,9},{7,10},{8,11},{9,12},{10... | collective-permute-start | bytes 786440 | tf_op jit(solution)/shard_map/ppermute | solution.py:17
  219.6 13.1 %collective-permute-start.11 = (f32[32,2048]{1,0:T(8,128)S(1)}, f32[32,2048]{1,0:T(8,128)S(1)}, u32[]{:S(2)}, u32[]{:S(2)}) collective-permute-start(f32[32,2048]{1,0:T(8,128)S(1)} %fusion.300), channel_id=1, source_target_pairs={{0,4},{1,5},{2,6},{3,7},{4,8},{5,9},{6,10},{7,11},{8,12},{9,13},{1... | collective-permute-start | bytes 786440 | tf_op jit(solution)/shard_map/ppermute | solution.py:17
where the time goes:
time: 235 us; the launch traced here: 233 us
  between operations  92.5 us (39%)
  matrix products  51.8 us (22%)
  starting transfers between devices  37.5 us (16%)
  blocking collectives  32.5 us (14%)
  local copies, waits for them, and re-layouts  11.1 us (5%)
  waiting for transfers between devices  4.06 us (2%)
  other arithmetic  3.96 us (2%)
    ppermute x12, starting transfers between devices, passed_along(): lax.ppermute(value, axis, [(source, source + steps) for source in range(f...  34.9 us
    dot_general x49, matrix products, kernel_block(): lax.dot_general(source, target, (((0,), (0,)), ((), ())), preferred_eleme...  20.8 us
    all_gather x1, blocking collectives, on_device(): gathered_roots = lax.all_gather(node_points[None], 'gx', axis=0, tiled=True)  17.5 us
    all_gather x1, blocking collectives, on_device(): lax.all_gather(node_weights[None], 'gx', axis=0, tiled=True)  14.9 us
    dot_general x48, matrix products, pair_terms(): lax.dot_general(high_values, kernel_tile, (((1,), (1,)), ((), ())), prefe...  12.2 us
    dot_general x48, matrix products, pair_terms(): jnp.dot(low_values, kernel_tile, preferred_element_type=jnp.float32)  9.1 us
    dot_general x4, matrix products, self_target(): jnp.dot(vectors, kernel_tile, preferred_element_type=jnp.float32)  6.01 us
  transfers between devices with their start and end apart: 16, of which 2 were waited for; matrix products, arithmetic and copies ran while one was open for 28% of the time, Pallas kernels for 0%

commit v1 on v0

--- a/solution.py
+++ b/solution.py
@@ -177,7 +177,10 @@
     node_potential = jnp.einsum(
         "n,ncs,nst->ct",
         far_flags,
-        lax.all_gather(node_weights[None], "gx", axis=0, tiled=True),
+        jnp.concatenate(
+            lax.all_to_all(jnp.stack([node_weights[None]] * lax.axis_size("gx")), "gx", 0, 0),
+            axis=0,
+        ),
         root_kernels,
         precision=lax.Precision.HIGHEST,
     )

time: 235 us -> 233 us (level)
  blocking collectives: 32.5 us -> 17.5 us
  waiting for transfers between devices: 4.06 us -> 9.48 us
  starting transfers between devices: 37.5 us -> 42.8 us
    all_gather x1 -> x0, blocking collectives: 14.9 us -> none  [on_device(): lax.all_gather(node_weights[None], 'gx', axis=0, tiled=True)]
    all_to_all x0 -> x1, waiting for transfers between devices: none -> 5.42 us  [on_device(): lax.all_to_all(jnp.stack([node_weights[None]] * lax.axis_size('gx')), 'gx...]
    all_to_all x0 -> x1, starting transfers between devices: none -> 4.71 us  [on_device(): lax.all_to_all(jnp.stack([node_weights[None]] * lax.axis_size('gx')), 'gx...]
  transfers between devices with their start and end apart: 16 -> 17, of which waited for: 2 -> 3; matrix products, arithmetic and copies ran while one was open for 28% -> 29% of each run, Pallas kernels for 0% -> 0%
where the time goes in v1:
time: 233 us; the launch traced here: 230 us
  between operations  92.5 us (40%)
  matrix products  51.8 us (22%)
  starting transfers between devices  42.8 us (18%)
  blocking collectives  17.5 us (8%)
  local copies, waits for them, and re-layouts  11.8 us (5%)
  waiting for transfers between devices  9.48 us (4%)
  other arithmetic  3.96 us (2%)
    ppermute x12, starting transfers between devices, passed_along(): lax.ppermute(value, axis, [(source, source + steps) for source in range(f...  35.6 us
    dot_general x49, matrix products, kernel_block(): lax.dot_general(source, target, (((0,), (0,)), ((), ())), preferred_eleme...  20.7 us
    all_gather x1, blocking collectives, on_device(): gathered_roots = lax.all_gather(node_points[None], 'gx', axis=0, tiled=True)  17.5 us
    dot_general x48, matrix products, pair_terms(): lax.dot_general(high_values, kernel_tile, (((1,), (1,)), ((), ())), prefe...  12.2 us
    dot_general x48, matrix products, pair_terms(): jnp.dot(low_values, kernel_tile, preferred_element_type=jnp.float32)  9.11 us
    dot_general x4, matrix products, self_target(): jnp.dot(vectors, kernel_tile, preferred_element_type=jnp.float32)  6.01 us
    all_to_all x1, waiting for transfers between devices, on_device(): lax.all_to_all(jnp.stack([node_weights[None]] * lax.axis_size('gx')), 'gx...  5.42 us
    all_to_all x1, starting transfers between devices, on_device(): lax.all_to_all(jnp.stack([node_weights[None]] * lax.axis_size('gx')), 'gx...  4.71 us
  transfers between devices with their start and end apart: 17, of which 3 were waited for; matrix products, arithmetic and copies ran while one was open for 29% of the time, Pallas kernels for 0%

profile of v1, /device:TPU:5, one launch (start us, length us, event | category | flops | bytes accessed | tf_op | source)
XLA Modules:
  0.0 229.9 jit_solution(6906976321797699625)
XLA Ops:
  0.0 3.2 %collective-permute-start.1 = (bf16[64,2048]{1,0:T(8,128)(2,1)}, bf16[64,2048]{1,0:T(8,128)(2,1)S(1)}, u32[]{:S(2)}, u32[]{:S(2)}) collective-permute-start(bf16[64,2048]{1,0:T(8,128)(2,1)} %param.15), channel_id=1, source_target_pairs={{1,0},{2,1},{3,2},{4,3},{5,4},{6,5},{7,6},{8,7},{9,8},{10,9},{11,1... | collective-permute-start | bytes 786440 | tf_op jit(solution)/shard_map/ppermute | solution.py:17
  3.2 3.7 %collective-permute-start.4 = (bf16[64,2048]{1,0:T(8,128)(2,1)}, bf16[64,2048]{1,0:T(8,128)(2,1)S(1)}, u32[]{:S(2)}, u32[]{:S(2)}) collective-permute-start(bf16[64,2048]{1,0:T(8,128)(2,1)} %param.15), channel_id=1, source_target_pairs={{2,0},{3,1},{4,2},{5,3},{6,4},{7,5},{8,6},{9,7},{10,8},{11,9},{12,... | collective-permute-start | bytes 786440 | tf_op jit(solution)/shard_map/ppermute | solution.py:17
  6.9 2.4 %collective-permute-start = (bf16[32,2048]{1,0:T(8,128)(2,1)}, bf16[32,2048]{1,0:T(8,128)(2,1)S(1)}, u32[]{:S(2)}, u32[]{:S(2)}) collective-permute-start(bf16[32,2048]{1,0:T(8,128)(2,1)} %param.16), channel_id=1, source_target_pairs={{1,0},{2,1},{3,2},{4,3},{5,4},{6,5},{7,6},{8,7},{9,8},{10,9},{11,1... | collective-permute-start | bytes 393224 | tf_op jit(solution)/shard_map/ppermute | solution.py:17
  9.4 1.9 collective-permute-start.3
  11.3 1.2 copy.31
  12.7 3.2 %gather_fusion.1 = bf16[512,64]{1,0:T(8,128)(2,1)S(1)} fusion(bf16[4,64,512]{1,2,0:T(8,128)(2,1)S(1)} %bitcast.343, s32[512]{0:T(512)S(1)} %fusion.382), kind=kCustom, calls=%fused_computation.3 | custom fusion | bytes 135168 | tf_op jit(solution)/shard_map/vmap(jit(_take))/gather | solution.py:44
  16.0 0.7 gather_fusion
  16.8 1.5 collective-permute-start.14
  18.3 0.7 fusion.395
  19.6 0.7 fusion.391
  22.3 0.7 fusion.392
  28.6 0.7 fusion.394
  52.0 0.7 fusion.393
  70.5 0.7 fusion.390
  112.8 6.5 %while.13 = (s32[]{:T(128)}, f32[32,2048]{1,0:T(8,128)S(1)}, bf16[64,2048]{1,0:T(8,128)(2,1)S(1)}, bf16[32,2048]{1,0:T(8,128)(2,1)S(1)}, s32[]{:T(128)}, /*index=5*/s32[]{:T(128)}, s32[]{:T(128)}, s32[]{:T(128)}) while((s32[]{:T(128)}, f32[32,2048]{1,0:T(8,128)S(1)}, bf16[64,2048]{1,0:T(8,128)(2,1)S(1)}, bf16[32,2048]{1,0:T(8,128)(2,1)S(1)}, ...), condition=%wide.region_3.0_spmd, body=%wide.region_0.0_spmd.sunk | while | flops 207058432 | bytes 873615 | solution.py:117
  112.9 1.5 fusion.504
  114.6 1.5 fusion.504
  116.2 1.5 fusion.504
  117.8 1.5 fusion.504
  119.5 0.7 convolution_bitcast_fusion.2
  122.3 0.7 gather_fusion.2
  123.1 1.7 collective-permute-done.12
  125.3 2.2 collective-permute-done.15
  127.6 0.7 collective-permute-start.13
  128.2 0.7 gather_fusion.3
  129.2 17.5 %all-gather = bf16[512,128]{1,0:T(8,128)(2,1)S(1)} all-gather(bf16[64,128]{1,0:T(8,128)(2,1)S(1)} %copy.32), channel_id=2, replica_groups=mesh['gx'=8,'gy'=4] {'gx'}, dimensions={0}, use_global_device_ids=true | all-gather | bytes 147456 | tf_op jit(solution)/shard_map/all_gather | solution.py:174
  146.8 2.6 %collective-permute-start.7 = (bf16[64,2048]{1,0:T(8,128)(2,1)S(1)}, bf16[64,2048]{1,0:T(8,128)(2,1)S(1)}, u32[]{:S(2)}, u32[]{:S(2)}) collective-permute-start(bf16[64,2048]{1,0:T(8,128)(2,1)S(1)} %get-tuple-element.348), channel_id=1, source_target_pairs={{3,0},{4,1},{5,2},{6,3},{7,4},{8,5},{9,6},{10,7},{11,8},{12,9},{13... | collective-permute-start | bytes 786440 | tf_op jit(solution)/shard_map/ppermute | solution.py:17
  149.6 0.7 stack.3
  150.3 4.7 %all-to-all-start = ((f32[8,1,32,128]{3,2,1,0:T(8,128)}), f32[8,1,32,128]{3,2,1,0:T(8,128)S(1)}, u32[]{:S(2)}, u32[]{:S(2)}) async-start(f32[8,1,32,128]{3,2,1,0:T(8,128)} %stack.3), calls=%async_computation | async-start | bytes 262144 | tf_op jit(solution)/shard_map/all_to_all | solution.py:181
  155.4 5.4 %all-to-all-done = f32[8,1,32,128]{3,2,1,0:T(8,128)S(1)} async-done(((f32[8,1,32,128]{3,2,1,0:T(8,128)}), f32[8,1,32,128]{3,2,1,0:T(8,128)S(1)}, u32[]{:S(2)}, u32[]{:S(2)}) %all-to-all-start) | async-done | bytes 131104 | tf_op jit(solution)/shard_map/all_to_all | solution.py:181
  161.5 4.0 %collective-permute-start.6 = (bf16[32,2048]{1,0:T(8,128)(2,1)S(1)}, bf16[32,2048]{1,0:T(8,128)(2,1)S(1)}, u32[]{:S(2)}, u32[]{:S(2)}) collective-permute-start(bf16[32,2048]{1,0:T(8,128)(2,1)S(1)} %get-tuple-element.353), channel_id=1, source_target_pairs={{3,0},{4,1},{5,2},{6,3},{7,4},{8,5},{9,6},{10,7},{11,8},{12,9},{13... | collective-permute-start | bytes 393224 | tf_op jit(solution)/shard_map/ppermute | solution.py:17
  166.4 0.4 fusion.202
  169.5 0.4 fusion.197
  170.2 0.4 fusion.196
  173.6 1.9 collective-permute-start.10
  176.4 0.4 fusion.190
  183.6 2.1 collective-permute-start.9
  189.8 0.4 fusion.173
  190.4 0.4 fusion.172
  192.3 0.4 fusion.169
  193.3 1.0 convolution_bitcast_fusion
  194.6 2.1 collective-permute-start.2
  200.8 0.4 fusion.161
  201.4 0.4 fusion.160
  204.5 5.0 %collective-permute-start.5 = (f32[32,2048]{1,0:T(8,128)S(1)}, f32[32,2048]{1,0:T(8,128)S(1)}, u32[]{:S(2)}, u32[]{:S(2)}) collective-permute-start(f32[32,2048]{1,0:T(8,128)S(1)} %fusion.256), channel_id=1, source_target_pairs={{0,2},{1,3},{2,4},{3,5},{4,6},{5,7},{6,8},{7,9},{8,10},{9,11},{10,... | collective-permute-start | bytes 786440 | tf_op jit(solution)/shard_map/ppermute | solution.py:17
  212.8 4.0 %collective-permute-start.8 = (f32[32,2048]{1,0:T(8,128)S(1)}, f32[32,2048]{1,0:T(8,128)S(1)}, u32[]{:S(2)}, u32[]{:S(2)}) collective-permute-start(f32[32,2048]{1,0:T(8,128)S(1)} %fusion.278), channel_id=1, source_target_pairs={{0,3},{1,4},{2,5},{3,6},{4,7},{5,8},{6,9},{7,10},{8,11},{9,12},{10... | collective-permute-start | bytes 786440 | tf_op jit(solution)/shard_map/ppermute | solution.py:17
  216.9 2.5 %collective-permute-start.11 = (f32[32,2048]{1,0:T(8,128)S(1)}, f32[32,2048]{1,0:T(8,128)S(1)}, u32[]{:S(2)}, u32[]{:S(2)}) collective-permute-start(f32[32,2048]{1,0:T(8,128)S(1)} %fusion.300), channel_id=1, source_target_pairs={{0,4},{1,5},{2,6},{3,7},{4,8},{5,9},{6,10},{7,11},{8,12},{9,13},{1... | collective-permute-start | bytes 786440 | tf_op jit(solution)/shard_map/ppermute | solution.py:17
  229.2 0.8 add_add_fusion
  (222 shorter events, 44.2 us)
Async XLA Ops:
  0.0 12.6 %copy-start.4 = (s32[4,128]{1,0:T(4,128)S(1)}, s32[4,128]{1,0:T(4,128)}, u32[]{:S(2)}) copy-start(s32[4,128]{1,0:T(4,128)} %param.17) | copy-start | bytes 6148
  0.0 12.6 %copy-start.8 = (s32[1,128]{1,0:T(1,128)S(1)}, s32[1,128]{1,0:T(1,128)}, u32[]{:S(2)}) copy-start(s32[1,128]{1,0:T(1,128)} %param.19) | copy-start | bytes 1540
  0.0 161.5 %collective-permute-start.1 = (bf16[64,2048]{1,0:T(8,128)(2,1)}, bf16[64,2048]{1,0:T(8,128)(2,1)S(1)}, u32[]{:S(2)}, u32[]{:S(2)}) collective-permute-start(bf16[64,2048]{1,0:T(8,128)(2,1)} %param.15), channel_id=1, source_target_pairs={{1,0},{2,1},{3,2},{4,3},{5,4},{6,5},{7,6},{8,7},{9,8},{10,9},{11,1... | collective-permute-start | bytes 786440 | tf_op jit(solution)/shard_map/ppermute | solution.py:17
  3.2 170.4 %collective-permute-start.4 = (bf16[64,2048]{1,0:T(8,128)(2,1)}, bf16[64,2048]{1,0:T(8,128)(2,1)S(1)}, u32[]{:S(2)}, u32[]{:S(2)}) collective-permute-start(bf16[64,2048]{1,0:T(8,128)(2,1)} %param.15), channel_id=1, source_target_pairs={{2,0},{3,1},{4,2},{5,3},{6,4},{7,5},{8,6},{9,7},{10,8},{11,9},{12,... | collective-permute-start | bytes 786440 | tf_op jit(solution)/shard_map/ppermute | solution.py:17
  6.9 197.6 %collective-permute-start = (bf16[32,2048]{1,0:T(8,128)(2,1)}, bf16[32,2048]{1,0:T(8,128)(2,1)S(1)}, u32[]{:S(2)}, u32[]{:S(2)}) collective-permute-start(bf16[32,2048]{1,0:T(8,128)(2,1)} %param.16), channel_id=1, source_target_pairs={{1,0},{2,1},{3,2},{4,3},{5,4},{6,5},{7,6},{8,7},{9,8},{10,9},{11,1... | collective-permute-start | bytes 393224 | tf_op jit(solution)/shard_map/ppermute | solution.py:17
  9.4 207.5 %collective-permute-start.3 = (bf16[32,2048]{1,0:T(8,128)(2,1)}, bf16[32,2048]{1,0:T(8,128)(2,1)S(1)}, u32[]{:S(2)}, u32[]{:S(2)}) collective-permute-start(bf16[32,2048]{1,0:T(8,128)(2,1)} %param.16), channel_id=1, source_target_pairs={{2,0},{3,1},{4,2},{5,3},{6,4},{7,5},{8,6},{9,7},{10,8},{11,9},{12,... | collective-permute-start | bytes 393224 | tf_op jit(solution)/shard_map/ppermute | solution.py:17
  12.6 4.1 %copy-start.7 = (s32[1,3,128]{2,0,1:T(1,128)S(1)}, s32[1,3,128]{2,0,1:T(1,128)}, u32[]{:S(2)}) copy-start(s32[1,3,128]{2,0,1:T(1,128)} %param.21) | copy-start | bytes 4612
  12.6 5.7 %copy-start.2 = (s32[1,4,12]{2,1,0:T(4,128)S(1)}, s32[1,4,12]{2,1,0:T(4,128)}, u32[]{:S(2)}) copy-start(s32[1,4,12]{2,1,0:T(4,128)} %param.24) | copy-start | bytes 580
  12.7 6.9 %copy-start.3 = (s32[1,4,12]{2,1,0:T(4,128)S(1)}, s32[1,4,12]{2,1,0:T(4,128)}, u32[]{:S(2)}) copy-start(s32[1,4,12]{2,1,0:T(4,128)} %param.25) | copy-start | bytes 580
  16.8 105.3 %collective-permute-start.14 = (bf16[64,128]{0,1:T(8,128)(2,1)S(1)}, bf16[64,128]{0,1:T(8,128)(2,1)S(1)}, u32[]{:S(2)}, u32[]{:S(2)}) collective-permute-start(bf16[64,128]{0,1:T(8,128)(2,1)S(1)} %select_bitcast_fusion.1), channel_id=1, source_target_pairs={{0,1},{1,0},{2,3},{3,2},{4,5},{5,4},{6,7},{7,6},{8,9},{9,8},{10,11... | collective-permute-start | bytes 49160 | tf_op jit(solution)/shard_map/ppermute | solution.py:23
  28.6 84.0 %copy-start.6 = (s32[1,3,256]{2,0,1:T(1,128)S(1)}, s32[1,3,256]{2,0,1:T(1,128)}, u32[]{:S(2)}) copy-start(s32[1,3,256]{2,0,1:T(1,128)} %param.22) | copy-start | bytes 9220
  29.4 83.4 %copy-start.10 = (s32[1,8]{1,0:T(1,128)S(1)}, s32[1,8]{1,0:T(1,128)}, u32[]{:S(2)}) copy-start(s32[1,8]{1,0:T(1,128)} %param.23) | copy-start | bytes 100
  50.6 62.2 %copy-start = (bf16[64,2048]{1,0:T(8,128)(2,1)S(1)}, bf16[64,2048]{1,0:T(8,128)(2,1)}, u32[]{:S(2)}) copy-start(bf16[64,2048]{1,0:T(8,128)(2,1)} %param.15) | copy-start | bytes 786436
  50.6 62.2 %copy-start.1 = (bf16[32,2048]{1,0:T(8,128)(2,1)S(1)}, bf16[32,2048]{1,0:T(8,128)(2,1)}, u32[]{:S(2)}) copy-start(bf16[32,2048]{1,0:T(8,128)(2,1)} %param.16) | copy-start | bytes 393220
  112.8 6.7 %copy-start.9 = (s32[4,512]{1,0:T(4,128)S(1)}, s32[4,512]{1,0:T(4,128)}, u32[]{:S(2)}) copy-start(s32[4,512]{1,0:T(4,128)} %param.18) | copy-start | bytes 24580
  119.3 0.9 copy-start.5
  122.1 2.7 %collective-permute-start.12 = (f32[32,128]{1,0:T(8,128)S(1)}, f32[32,128]{1,0:T(8,128)S(1)}, u32[]{:S(2)}, u32[]{:S(2)}) collective-permute-start(f32[32,128]{1,0:T(8,128)S(1)} %fusion.303), channel_id=1, source_target_pairs={{0,1},{1,0},{2,3},{3,2},{4,5},{5,4},{6,7},{7,6},{8,9},{9,8},{10,11... | collective-permute-start | bytes 49160 | tf_op jit(solution)/shard_map/ppermute | solution.py:23
  124.8 2.8 %collective-permute-start.15 = (bf16[64,128]{0,1:T(8,128)(2,1)S(1)}, bf16[64,128]{0,1:T(8,128)(2,1)S(1)}, u32[]{:S(2)}, u32[]{:S(2)}) collective-permute-start(bf16[64,128]{0,1:T(8,128)(2,1)S(1)} %select_bitcast_fusion), channel_id=1, source_target_pairs={{0,2},{1,3},{2,0},{3,1},{4,6},{5,7},{6,4},{7,5},{8,10},{9,11},{10,... | collective-permute-start | bytes 49160 | tf_op jit(solution)/shard_map/ppermute | solution.py:23
  127.6 19.3 %collective-permute-start.13 = (f32[32,128]{1,0:T(8,128)S(1)}, f32[32,128]{1,0:T(8,128)S(1)}, u32[]{:S(2)}, u32[]{:S(2)}) collective-permute-start(f32[32,128]{1,0:T(8,128)S(1)} %fusion.309), channel_id=1, source_target_pairs={{0,2},{1,3},{2,0},{3,1},{4,6},{5,7},{6,4},{7,5},{8,10},{9,11},{10,... | collective-permute-start | bytes 49160 | tf_op jit(solution)/shard_map/ppermute | solution.py:23
  146.8 36.8 %collective-permute-start.7 = (bf16[64,2048]{1,0:T(8,128)(2,1)S(1)}, bf16[64,2048]{1,0:T(8,128)(2,1)S(1)}, u32[]{:S(2)}, u32[]{:S(2)}) collective-permute-start(bf16[64,2048]{1,0:T(8,128)(2,1)S(1)} %get-tuple-element.348), channel_id=1, source_target_pairs={{3,0},{4,1},{5,2},{6,3},{7,4},{8,5},{9,6},{10,7},{11,8},{12,9},{13... | collective-permute-start | bytes 786440 | tf_op jit(solution)/shard_map/ppermute | solution.py:17
  150.3 10.5 %all-to-all-start = ((f32[8,1,32,128]{3,2,1,0:T(8,128)}), f32[8,1,32,128]{3,2,1,0:T(8,128)S(1)}, u32[]{:S(2)}, u32[]{:S(2)}) async-start(f32[8,1,32,128]{3,2,1,0:T(8,128)} %stack.3), calls=%async_computation | async-start | bytes 262144 | tf_op jit(solution)/shard_map/all_to_all | solution.py:181
  161.5 61.1 %collective-permute-start.6 = (bf16[32,2048]{1,0:T(8,128)(2,1)S(1)}, bf16[32,2048]{1,0:T(8,128)(2,1)S(1)}, u32[]{:S(2)}, u32[]{:S(2)}) collective-permute-start(bf16[32,2048]{1,0:T(8,128)(2,1)S(1)} %get-tuple-element.353), channel_id=1, source_target_pairs={{3,0},{4,1},{5,2},{6,3},{7,4},{8,5},{9,6},{10,7},{11,8},{12,9},{13... | collective-permute-start | bytes 393224 | tf_op jit(solution)/shard_map/ppermute | solution.py:17
  173.6 21.0 %collective-permute-start.10 = (bf16[64,2048]{1,0:T(8,128)(2,1)S(1)}, bf16[64,2048]{1,0:T(8,128)(2,1)S(1)}, u32[]{:S(2)}, u32[]{:S(2)}) collective-permute-start(bf16[64,2048]{1,0:T(8,128)(2,1)S(1)} %get-tuple-element.348), channel_id=1, source_target_pairs={{4,0},{5,1},{6,2},{7,3},{8,4},{9,5},{10,6},{11,7},{12,8},{13,9},{1... | collective-permute-start | bytes 786440 | tf_op jit(solution)/shard_map/ppermute | solution.py:17
  183.6 42.3 %collective-permute-start.9 = (bf16[32,2048]{1,0:T(8,128)(2,1)S(1)}, bf16[32,2048]{1,0:T(8,128)(2,1)S(1)}, u32[]{:S(2)}, u32[]{:S(2)}) collective-permute-start(bf16[32,2048]{1,0:T(8,128)(2,1)S(1)} %get-tuple-element.353), channel_id=1, source_target_pairs={{4,0},{5,1},{6,2},{7,3},{8,4},{9,5},{10,6},{11,7},{12,8},{13,9},{1... | collective-permute-start | bytes 393224 | tf_op jit(solution)/shard_map/ppermute | solution.py:17
  194.6 18.1 %collective-permute-start.2 = (f32[32,2048]{1,0:T(8,128)S(1)}, f32[32,2048]{1,0:T(8,128)S(1)}, u32[]{:S(2)}, u32[]{:S(2)}) collective-permute-start(f32[32,2048]{1,0:T(8,128)S(1)} %fusion.234), channel_id=1, source_target_pairs={{0,1},{1,2},{2,3},{3,4},{4,5},{5,6},{6,7},{7,8},{8,9},{9,10},{10,1... | collective-permute-start | bytes 786440 | tf_op jit(solution)/shard_map/ppermute | solution.py:17
  204.5 18.1 %collective-permute-start.5 = (f32[32,2048]{1,0:T(8,128)S(1)}, f32[32,2048]{1,0:T(8,128)S(1)}, u32[]{:S(2)}, u32[]{:S(2)}) collective-permute-start(f32[32,2048]{1,0:T(8,128)S(1)} %fusion.256), channel_id=1, source_target_pairs={{0,2},{1,3},{2,4},{3,5},{4,6},{5,7},{6,8},{7,9},{8,10},{9,11},{10,... | collective-permute-start | bytes 786440 | tf_op jit(solution)/shard_map/ppermute | solution.py:17
  212.8 13.1 %collective-permute-start.8 = (f32[32,2048]{1,0:T(8,128)S(1)}, f32[32,2048]{1,0:T(8,128)S(1)}, u32[]{:S(2)}, u32[]{:S(2)}) collective-permute-start(f32[32,2048]{1,0:T(8,128)S(1)} %fusion.278), channel_id=1, source_target_pairs={{0,3},{1,4},{2,5},{3,6},{4,7},{5,8},{6,9},{7,10},{8,11},{9,12},{10... | collective-permute-start | bytes 786440 | tf_op jit(solution)/shard_map/ppermute | solution.py:17
  216.9 12.3 %collective-permute-start.11 = (f32[32,2048]{1,0:T(8,128)S(1)}, f32[32,2048]{1,0:T(8,128)S(1)}, u32[]{:S(2)}, u32[]{:S(2)}) collective-permute-start(f32[32,2048]{1,0:T(8,128)S(1)} %fusion.300), channel_id=1, source_target_pairs={{0,4},{1,5},{2,6},{3,7},{4,8},{5,9},{6,10},{7,11},{8,12},{9,13},{1... | collective-permute-start | bytes 786440 | tf_op jit(solution)/shard_map/ppermute | solution.py:17
